TPU v7x, 32 devices: a whole 2x2x4 slice. The times are simulated.
32 devices in a mesh: dp: 4 (over z), lib: 8 (over y, x, core).
Axes of the slice: x: 2, y: 2, z: 4, core: 2. Of those that a mesh axis runs over, the one named last changes fastest.
Arguments:
- spectra: bfloat16 [12288, 512], P(('dp', 'lib')), may hold values from -6 to 6
- w_proj: bfloat16 [512, 512], replicated, may hold values from -0.25 to 0.25
- fixed_library_matrix: bfloat16 [8192, 512], P('lib')
- mol_rows: bfloat16 [65536, 512], P(('dp', 'lib'))
- cand_ids: int32 [12288, 4], P(('dp', 'lib')), may hold values from 0 to 65535, as said below
- iso_count: int32 [12288], P(('dp', 'lib')), may hold values from 1 to 3
Outputs:
- grad_w: float32 [512, 512], replicated
- grad_mol: float32 [65536, 512], P(('dp', 'lib'))
- loss: float32 [], replicated
Inputs may be any that keep to these rules, and one draw needn't show every extreme that they name: cand_ids of a spectrum on device dp, lib (in dp+lib order) name rows of the dp group's molecules: id // 2048 // 8 equals dp. Over one device's 1536 slots (all columns, live or not), at most 384 name rows whose (id // 2048) % 8 is one lib index, and exactly 384 for some lib index on every device.
All inputs are finite; a program needn't handle non-finite values.
Results may differ from a plain program's by a relative error of at most 0.0074.
Values may be sent and summed in bfloat16 or wider, within the bound.
No kernel may reach another device: no remote copies, remote signals or barrier semaphores. Data moves between devices by JAX's collectives and lax.ppermute only.
A program may use at most 64 MiB of HBM per device.

v0:
```python
import jax
import jax.numpy as jnp
from jax import lax
from jax.sharding import PartitionSpec as P

sharpness_divisor = 0.07


def absorb(state, block, spectrum_encoding):
    running_max, running_sum, derivative_tally = state
    scores = (
        lax.dot_general(
            spectrum_encoding, block, (((1,), (1,)), ((), ())), preferred_element_type=jnp.float32
        )
        / sharpness_divisor
    )
    new_max = jnp.maximum(running_max, jnp.max(scores, axis=1))
    inverse_sharpness = jnp.exp(running_max - new_max)
    weights = jnp.exp(scores - new_max[:, None])
    running_sum = running_sum * inverse_sharpness + jnp.sum(weights, axis=1)
    derivative_tally = derivative_tally * inverse_sharpness[:, None] + jnp.dot(
        weights.astype(jnp.bfloat16), block, preferred_element_type=jnp.float32
    )
    return (new_max, running_sum, derivative_tally)


def per_device(spectra, w_proj, fixed_library_matrix, mol_rows, cand_ids, iso_count):
    q_rows = spectra.shape[0]
    width = spectra.shape[1]
    mol_count = mol_rows.shape[0]
    bank_count = fixed_library_matrix.shape[0]
    lib_size = lax.axis_size("lib")
    columns = cand_ids.shape[1]
    slot_count = q_rows * columns
    capacity = 2 * slot_count // lib_size
    u_proj = jnp.dot(spectra, w_proj, preferred_element_type=jnp.float32)
    norm = jnp.sqrt(jnp.sum(u_proj * u_proj, axis=1, keepdims=True) + 1e-06)
    normalized_spectrum_matrix = u_proj / norm
    spectrum_encoding = normalized_spectrum_matrix.astype(jnp.bfloat16)
    flat_ids = cand_ids.reshape(-1)
    owner = flat_ids // mol_count % lib_size
    local_row = flat_ids % mol_count
    onehot = (owner[:, None] == jnp.arange(lib_size, dtype=jnp.int32)[None, :]).astype(jnp.int32)
    before = jnp.cumsum(onehot, axis=0) - onehot
    position = owner * capacity + jnp.sum(before * onehot, axis=1)
    requests = jnp.zeros((lib_size * capacity,), jnp.int32).at[position].set(local_row)
    requests = requests.reshape(lib_size, capacity)
    received = lax.all_to_all(requests, "lib", split_axis=0, concat_axis=0, tiled=True)
    fetched = mol_rows[received]
    returned = lax.all_to_all(fetched, "lib", split_axis=0, concat_axis=0, tiled=True)
    contender_embedding_matrix = returned.reshape(lib_size * capacity, width)[position].reshape(
        q_rows, columns, width
    )
    candidate_float_rows = contender_embedding_matrix.astype(jnp.float32)
    column = jnp.arange(columns, dtype=jnp.int32)[None, :]
    live = column <= iso_count[:, None]
    contender_similarity_values = (
        jnp.einsum(
            "ti,tmi->tm",
            spectrum_encoding,
            contender_embedding_matrix,
            preferred_element_type=jnp.float32,
        )
        / sharpness_divisor
    )
    cand_max = jnp.max(jnp.where(live, contender_similarity_values, -1e30), axis=1)
    cand_weights = jnp.where(live, jnp.exp(contender_similarity_values - cand_max[:, None]), 0.0)
    start_state = (
        cand_max,
        jnp.sum(cand_weights, axis=1),
        jnp.einsum("qk,qkd->qd", cand_weights, candidate_float_rows),
    )
    piece = lax.all_gather(fixed_library_matrix, "lib", axis=0, tiled=True)
    stacked = piece.reshape(piece.shape[0] // bank_count, bank_count, width)

    def inner(current, block):
        return (absorb(current, block, spectrum_encoding), 0)

    result, unused = lax.scan(inner, start_state, stacked)
    top, objective_aggregate, derivative_tally = result
    lse = top + jnp.log(objective_aggregate)
    scaled_cand = jnp.where(live, jnp.exp(contender_similarity_values - top[:, None]), 0.0)
    loss_terms = jnp.sum(lse - contender_similarity_values[:, 0])
    spectrum_derivative = (
        derivative_tally / objective_aggregate[:, None] - candidate_float_rows[:, 0, :]
    ) / sharpness_divisor
    grad_u = (
        (
            spectrum_derivative
            - normalized_spectrum_matrix
            * jnp.sum(normalized_spectrum_matrix * spectrum_derivative, axis=1, keepdims=True)
        )
        / norm
    ).astype(jnp.bfloat16)
    grad_local = jnp.dot(spectra.T, grad_u, preferred_element_type=jnp.float32)
    first = (column == 0).astype(jnp.float32)
    inverse_sharpness = jnp.where(live, scaled_cand / objective_aggregate[:, None] - first, 0.0)
    contender_derivative = (
        inverse_sharpness[:, :, None] * normalized_spectrum_matrix[:, None, :] / sharpness_divisor
    ).astype(jnp.bfloat16)
    outgoing = (
        jnp.zeros((lib_size * capacity, width), jnp.bfloat16)
        .at[position]
        .set(contender_derivative.reshape(slot_count, width))
    )
    incoming = lax.all_to_all(
        outgoing.reshape(lib_size, capacity, width), "lib", split_axis=0, concat_axis=0, tiled=True
    )
    grad_mol = (
        jnp.zeros((mol_count, width), jnp.float32)
        .at[received.reshape(-1)]
        .add(incoming.reshape(-1, width).astype(jnp.float32))
    )
    grad_w, loss_sum = lax.psum((grad_local, loss_terms), ("dp", "lib"))
    loss = loss_sum / (q_rows * lax.axis_size("dp") * lib_size)
    return (grad_w, grad_mol, loss)


def solution(mesh):
    placed = (
        P(("dp", "lib"), None),
        P(),
        P("lib", None),
        P(("dp", "lib"), None),
        P(("dp", "lib"), None),
        P(("dp", "lib")),
    )
    return jax.shard_map(
        per_device,
        mesh=mesh,
        in_specs=placed,
        out_specs=(P(), P(("dp", "lib"), None), P()),
        check_vma=False,
    )
```

profile of v0, /device:TPU:0, one launch (start us, length us, event | category | flops | bytes accessed | tf_op | source)
XLA Modules:
  0.0 341.9 jit_solution(17671516270576667808)
XLA Ops:
  7.2 0.7 all-gather.2.cloned.1.call-update
  7.9 0.8 copy.10
  8.7 0.1 reshape.271
  8.9 0.1 reshape.270
  9.0 0.1 reshape.269
  9.2 2.3 reduce-window.6
  11.5 0.3 slice_reduce_fusion
  11.8 0.2 reduce-window.9
  12.0 0.1 add_bitcast_fusion
  12.1 0.1 fusion.31
  12.2 6.2 %scatter_custom_fusion = s32[3072]{0:T(1024)S(1)} fusion(s32[1536]{0:T(1024)S(1)} %fusion.31, s32[1536]{0:T(1024)S(1)} %get-tuple-element.64, s32[]{:T(128)} %copy.49), kind=kCustom, calls=%fused_computation.91 | custom fusion | bytes 12292 | tf_op jit(solution)/shard_map/scatter | solution.py:46
  18.4 10.0 %all_to_all.22 = s32[8,1,384]{2,1,0:T(1,128)S(1)} all-to-all(s32[8,1,384]{2,1,0:T(1,128)S(1)} %bitcast.85), channel_id=1, replica_groups=mesh['dp'=4,'lib'=8] {'lib'}, dimensions={0} | all-to-all | bytes 24576 | tf_op jit(solution)/shard_map/all_to_all | solution.py:48
  28.4 13.3 %gather_fusion = bf16[3072,512]{1,0:T(8,128)(2,1)} fusion(bf16[2048,512]{1,0:T(8,128)(2,1)S(1)} %copy-done, s32[3072]{0:T(1024)S(1)} %broadcast_clamp_fusion), kind=kCustom, calls=%fused_computation | custom fusion | bytes 6303744 | tf_op jit(solution)/shard_map/gather | solution.py:49
  41.7 4.8 %all-to-all-start.1 = ((bf16[8,384,512]{2,1,0:T(8,128)(2,1)}), bf16[8,384,512]{2,1,0:T(8,128)(2,1)}, u32[]{:S(2)}, u32[]{:S(2)}) async-start(bf16[8,384,512]{2,1,0:T(8,128)(2,1)} %bitcast.83), calls=%async_computation.1 | async-start | bytes 6291456 | tf_op jit(solution)/shard_map/all_to_all | solution.py:50
  46.5 0.5 multiply_reduce_fusion.1
  47.0 0.2 fusion.41
  47.1 0.9 copy-done.1
  48.0 2.2 mul.68
  50.2 4.9 %mul.69 = f32[1536,512]{1,0:T(8,128)} reshape(f32[384,4,512]{2,1,0:T(4,128)} %mul.68) | data formatting | bytes 6291456 | tf_op jit(solution)/shard_map/mul | solution.py:99
  55.1 44.7 %all-to-all-done.1 = bf16[8,384,512]{2,1,0:T(8,128)(2,1)} async-done(((bf16[8,384,512]{2,1,0:T(8,128)(2,1)}), bf16[8,384,512]{2,1,0:T(8,128)(2,1)}, u32[]{:S(2)}, u32[]{:S(2)}) %all-to-all-start.1) | async-done | bytes 3145760 | tf_op jit(solution)/shard_map/all_to_all | solution.py:50
  99.8 7.8 %gather_fusion.1 = bf16[1536,512]{1,0:T(8,128)(2,1)} fusion(bf16[3072,512]{1,0:T(8,128)(2,1)} %bitcast.7, s32[2048]{0:T(1024)S(1)} %pad_clamp_fusion), kind=kCustom, calls=%fused_computation.1 | custom fusion | bytes 3151872 | tf_op jit(solution)/shard_map/gather | solution.py:51
  107.6 3.5 %reshape.274 = bf16[384,4,512]{2,1,0:T(4,128)(2,1)} reshape(bf16[1536,512]{1,0:T(8,128)(2,1)} %gather_fusion.1) | data formatting | bytes 3145728 | tf_op jit(solution)/shard_map/reshape | solution.py:51
  111.1 2.8 fusion.18
  113.9 0.1 copy.17
  114.1 0.2 copy.18
  114.3 2.4 fusion.43
  116.8 34.0 %while.14 = (s32[]{:T(128)}, f32[384]{0:T(512)S(1)}, f32[384]{0:T(512)S(1)}, f32[384,512]{1,0:T(8,128)S(1)}, bf16[8,1024,512]{2,1,0:T(8,128)(2,1)}, /*index=5*/bf16[384,512]{1,0:T(8,128)(2,1)S(1)}, s32[]{:T(128)}) while((s32[]{:T(128)}, f32[384]{0:T(512)S(1)}, f32[384]{0:T(512)S(1)}, f32[384,512]{1,0:T(8,128)S(1)}, ...), condition=%wide.region_10.11_spmd, body=%wide.region_7.10_spmd.sunk | while | flops 808059648 | bytes 8806493 | solution.py:79
  116.8 2.0 fusion.59
  118.8 0.3 fusion.60
  119.1 1.9 convolution_add_fusion.2
  121.1 2.0 fusion.59
  123.0 0.3 fusion.60
  123.3 1.9 convolution_add_fusion.2
  125.3 2.0 fusion.59
  127.3 0.3 fusion.60
  127.6 1.9 convolution_add_fusion.2
  129.6 2.0 fusion.59
  131.5 0.3 fusion.60
  131.8 1.9 convolution_add_fusion.2
  133.8 2.0 fusion.59
  135.8 0.3 fusion.60
  136.1 1.9 convolution_add_fusion.2
  138.1 2.0 fusion.59
  140.0 0.3 fusion.60
  140.4 1.9 convolution_add_fusion.2
  142.3 2.0 fusion.59
  144.3 0.3 fusion.60
  144.6 1.9 convolution_add_fusion.2
  146.6 2.0 fusion.59
  148.5 0.3 fusion.60
  148.9 1.9 convolution_add_fusion.2
  150.9 0.1 copy.14
  151.0 0.1 mul.66
  151.2 10.7 %scatter_custom_fusion.1 = bf16[3072,512]{1,0:T(8,128)(2,1)} fusion(s32[1536]{0:T(1024)S(1)} %fusion.31, f32[1536,512]{1,0:T(8,128)} %mul.69, f32[]{:T(128)} %constant.84.clone.1, f32[1536]{0:T(1024)S(1)} %mul.66, bf16[]{:T(256)} %constant.87.clone.1), kind=kCustom, calls=%fused_computation.23 | custom fusion | flops 2359296 | bytes 6299654 | tf_op jit(solution)/shard_map/scatter | solution.py:104
  161.9 4.4 %all-to-all-start.2 = ((bf16[8,384,512]{2,1,0:T(8,128)(2,1)}), bf16[8,384,512]{2,1,0:T(8,128)(2,1)}, u32[]{:S(2)}, u32[]{:S(2)}) async-start(bf16[8,384,512]{2,1,0:T(8,128)(2,1)} %bitcast.82), calls=%async_computation.2 | async-start | bytes 6291456 | tf_op jit(solution)/shard_map/all_to_all | solution.py:106
  166.3 0.3 all-reduce.2.cloned.1.call-start
  166.6 2.0 slice.22
  168.7 1.4 multiply_reduce_fusion
  170.1 1.7 convolution_bitcast_fusion
  171.8 0.6 subtract_reduce_fusion
  172.5 67.0 %psum.15 = f32[]{:T(128)} all-reduce(f32[]{:T(128)} %subtract_reduce_fusion), channel_id=1, replica_groups=mesh['dp'=4,'lib'=8] {'dp','lib'}, use_global_device_ids=true, to_apply=%region_16.17 | all-reduce | flops 1 | bytes 8 | tf_op jit(solution)/shard_map/psum | solution.py:114
  240.2 68.1 %all-reduce.2.cloned.1.call-done = f32[512,512]{0,1:T(8,128)} async-done(((f32[512,512]{0,1:T(8,128)}), f32[512,512]{0,1:T(8,128)}) %all-reduce.2.cloned.1.call-update) | async-done | bytes 1048592 | tf_op jit(solution)/shard_map/psum | solution.py:114
  308.2 2.5 copy.15
  310.7 23.2 %scatter_custom_fusion.2 = f32[2048,512]{1,0:T(8,128)} fusion(s32[3072]{0:T(1024)S(1)} %bitcast.88, bf16[3072,512]{1,0:T(8,128)(2,1)} %bitcast.19, f32[]{:T(128)} %constant.73.clone.1), kind=kCustom, calls=%fused_computation.19 | custom fusion | flops 3145728 | bytes 7340036 | tf_op jit(solution)/shard_map/scatter-add | solution.py:112
  (57 shorter events, 0.6 us)
Async XLA Ops:
  7.2 21.2 %copy-start = (bf16[2048,512]{1,0:T(8,128)(2,1)S(1)}, bf16[2048,512]{1,0:T(8,128)(2,1)}, u32[]{:S(2)}) copy-start(bf16[2048,512]{1,0:T(8,128)(2,1)} %param.11) | copy-start | bytes 6291460
  7.2 109.6 %all-gather.2.cloned.1.call-start = ((), (), s32[]{:S(2)}) async-start(), calls=%async_computation.3 | async-start | bytes 9437184 | tf_op jit(solution)/shard_map/all_gather | solution.py:73
  41.7 4.8 %copy-start.3 = (bf16[512,512]{1,0:T(8,128)(2,1)S(1)}, bf16[512,512]{1,0:T(8,128)(2,1)}, u32[]{:S(2)}) copy-start(bf16[512,512]{1,0:T(8,128)(2,1)} %param.9) | copy-start | bytes 1572868
  41.7 4.8 %copy-start.4 = (bf16[384,512]{1,0:T(8,128)(2,1)S(1)}, bf16[384,512]{1,0:T(8,128)(2,1)}, u32[]{:S(2)}) copy-start(bf16[384,512]{1,0:T(8,128)(2,1)} %param.8) | copy-start | bytes 1179652
  41.7 58.1 %all-to-all-start.1 = ((bf16[8,384,512]{2,1,0:T(8,128)(2,1)}), bf16[8,384,512]{2,1,0:T(8,128)(2,1)}, u32[]{:S(2)}, u32[]{:S(2)}) async-start(bf16[8,384,512]{2,1,0:T(8,128)(2,1)} %bitcast.83), calls=%async_computation.1 | async-start | bytes 6291456 | tf_op jit(solution)/shard_map/all_to_all | solution.py:50
  47.1 0.9 copy-start.1
  111.1 2.9 copy-start.6
  161.9 148.9 %all-to-all-start.2 = ((bf16[8,384,512]{2,1,0:T(8,128)(2,1)}), bf16[8,384,512]{2,1,0:T(8,128)(2,1)}, u32[]{:S(2)}, u32[]{:S(2)}) async-start(bf16[8,384,512]{2,1,0:T(8,128)(2,1)} %bitcast.82), calls=%async_computation.2 | async-start | bytes 6291456 | tf_op jit(solution)/shard_map/all_to_all | solution.py:106
  166.3 3.8 %copy-start.5 = (bf16[384,512]{1,0:T(8,128)(2,1)S(1)}, bf16[384,512]{1,0:T(8,128)(2,1)}, u32[]{:S(2)}) copy-start(bf16[384,512]{1,0:T(8,128)(2,1)} %param.8) | copy-start | bytes 1179652
  166.3 141.9 %all-reduce.2.cloned.1.call-start = ((), (), s32[]{:S(2)}) async-start(), calls=%async_computation.4 | async-start | bytes 2097152 | tf_op jit(solution)/shard_map/psum | solution.py:114
  166.6 3.5 %copy-start.2 = (f32[384,512]{1,0:T(8,128)S(1)}, f32[384,512]{1,0:T(8,128)}, u32[]{:S(2)}) copy-start(f32[384,512]{1,0:T(8,128)} %copy-done.1) | copy-start | bytes 2359300
Sparse Core Ops, SparseCore 0:
  9.9 81.2 all-gather.1
  172.9 135.2 all-reduce.1
where the time goes:
time: 343 us; the launch traced here: 342 us
  waiting for transfers between devices  113 us (33%)
  blocking collectives  77 us (22%)
  local copies, waits for them, and re-layouts  45.5 us (13%)
  other arithmetic  41.5 us (12%)
  matrix products  38.6 us (11%)
  between operations  16.1 us (5%)
  starting transfers between devices  9.51 us (3%)
    psum x1, waiting for transfers between devices, per_device(): grad_w, loss_sum = lax.psum((grad_local, loss_terms), ('dp', 'lib'))  68.1 us
    psum x1, blocking collectives, per_device(): grad_w, loss_sum = lax.psum((grad_local, loss_terms), ('dp', 'lib'))  67 us
    all_to_all x1, waiting for transfers between devices, per_device(): lax.all_to_all(fetched, 'lib', split_axis=0, concat_axis=0, tiled=True)  44.7 us
    scatter-add x1, other arithmetic, per_device(): grad_mol = jnp.zeros((mol_count, width), jnp.float32).at[received.reshape...  23.2 us
    dot_general x8, matrix products, absorb(): lax.dot_general(spectrum_encoding, block, (((1,), (1,)), ((), ())), prefe...  15.7 us
    dot_general x8, matrix products, absorb(): jnp.dot(weights.astype(jnp.bfloat16), block, preferred_element_type=jnp.f...  15.5 us
    gather x1, local copies, waits for them, and re-layouts, per_device(): fetched = mol_rows[received]  13.3 us
    scatter x1, other arithmetic, per_device(): outgoing = jnp.zeros((lib_size * capacity, width), jnp.bfloat16).at[posit...  10.7 us
  transfers between devices with their start and end apart: 4, of which 2 were waited for; matrix products, arithmetic and copies ran while one was open for 17% of the time, Pallas kernels for 0%

commit v1 on v0

--- a/solution.py
+++ b/solution.py
@@ -111,7 +111,7 @@
         .at[received.reshape(-1)]
         .add(incoming.reshape(-1, width).astype(jnp.float32))
     )
-    grad_w, loss_sum = lax.psum((grad_local, loss_terms), ("dp", "lib"))
+    grad_w, loss_sum = lax.psum(lax.psum((grad_local, loss_terms), "lib"), "dp")
     loss = loss_sum / (q_rows * lax.axis_size("dp") * lib_size)
     return (grad_w, grad_mol, loss)
 

time: 343 us -> 329 us (0.959)
  blocking collectives: 77 us -> 35.6 us
  waiting for transfers between devices: 113 us -> 141 us
    psum x1 -> x2, blocking collectives: 67 us -> 25.6 us  [per_device(): grad_w, loss_sum = lax.psum(lax.psum((grad_local, loss_terms), 'lib'), 'dp')]
    psum x1 -> x2, waiting for transfers between devices: 68.1 us -> 95.8 us  [per_device(): grad_w, loss_sum = lax.psum(lax.psum((grad_local, loss_terms), 'lib'), 'dp')]
  transfers between devices with their start and end apart: 4 -> 5, of which waited for: 2 -> 3; matrix products, arithmetic and copies ran while one was open for 17% -> 17% of each run, Pallas kernels for 0% -> 0%
where the time goes in v1:
time: 329 us; the launch traced here: 328 us
  waiting for transfers between devices  141 us (43%)
  local copies, waits for them, and re-layouts  45.5 us (14%)
  other arithmetic  41.5 us (13%)
  matrix products  38.6 us (12%)
  blocking collectives  35.6 us (11%)
  between operations  15.8 us (5%)
  starting transfers between devices  9.55 us (3%)
    psum x2, waiting for transfers between devices, per_device(): grad_w, loss_sum = lax.psum(lax.psum((grad_local, loss_terms), 'lib'), 'dp')  95.8 us
    all_to_all x1, waiting for transfers between devices, per_device(): lax.all_to_all(fetched, 'lib', split_axis=0, concat_axis=0, tiled=True)  44.7 us
    psum x2, blocking collectives, per_device(): grad_w, loss_sum = lax.psum(lax.psum((grad_local, loss_terms), 'lib'), 'dp')  25.6 us
    scatter-add x1, other arithmetic, per_device(): grad_mol = jnp.zeros((mol_count, width), jnp.float32).at[received.reshape...  23.2 us
    dot_general x8, matrix products, absorb(): lax.dot_general(spectrum_encoding, block, (((1,), (1,)), ((), ())), prefe...  15.7 us
    dot_general x8, matrix products, absorb(): jnp.dot(weights.astype(jnp.bfloat16), block, preferred_element_type=jnp.f...  15.5 us
    gather x1, local copies, waits for them, and re-layouts, per_device(): fetched = mol_rows[received]  13.3 us
    scatter x1, other arithmetic, per_device(): outgoing = jnp.zeros((lib_size * capacity, width), jnp.bfloat16).at[posit...  10.7 us
  transfers between devices with their start and end apart: 5, of which 3 were waited for; matrix products, arithmetic and copies ran while one was open for 17% of the time, Pallas kernels for 0%

profile of v1, /device:TPU:0, one launch (start us, length us, event | category | flops | bytes accessed | tf_op | source)
XLA Modules:
  0.0 328.0 jit_solution(2424028849979133578)
XLA Ops:
  7.2 0.7 all-gather.2.cloned.1.call-update
  7.9 0.8 copy.10
  8.7 0.1 reshape.271
  8.9 0.1 reshape.270
  9.0 0.1 reshape.269
  9.2 2.3 reduce-window.6
  11.5 0.3 slice_reduce_fusion
  11.8 0.2 reduce-window.9
  12.2 6.2 %scatter_custom_fusion = s32[3072]{0:T(1024)S(1)} fusion(s32[1536]{0:T(1024)S(1)} %fusion.31, s32[1536]{0:T(1024)S(1)} %get-tuple-element.64, s32[]{:T(128)} %copy.50), kind=kCustom, calls=%fused_computation.91 | custom fusion | bytes 12292 | tf_op jit(solution)/shard_map/scatter | solution.py:46
  18.4 10.0 %all_to_all.22 = s32[8,1,384]{2,1,0:T(1,128)S(1)} all-to-all(s32[8,1,384]{2,1,0:T(1,128)S(1)} %bitcast.85), channel_id=1, replica_groups=mesh['dp'=4,'lib'=8] {'lib'}, dimensions={0} | all-to-all | bytes 24576 | tf_op jit(solution)/shard_map/all_to_all | solution.py:48
  28.4 13.3 %gather_fusion = bf16[3072,512]{1,0:T(8,128)(2,1)} fusion(bf16[2048,512]{1,0:T(8,128)(2,1)S(1)} %copy-done, s32[3072]{0:T(1024)S(1)} %broadcast_clamp_fusion), kind=kCustom, calls=%fused_computation | custom fusion | bytes 6303744 | tf_op jit(solution)/shard_map/gather | solution.py:49
  41.7 4.8 %all-to-all-start.1 = ((bf16[8,384,512]{2,1,0:T(8,128)(2,1)}), bf16[8,384,512]{2,1,0:T(8,128)(2,1)}, u32[]{:S(2)}, u32[]{:S(2)}) async-start(bf16[8,384,512]{2,1,0:T(8,128)(2,1)} %bitcast.83), calls=%async_computation.1 | async-start | bytes 6291456 | tf_op jit(solution)/shard_map/all_to_all | solution.py:50
  46.5 0.5 multiply_reduce_fusion.1
  47.0 0.2 fusion.41
  47.1 0.9 copy-done.1
  48.0 2.2 mul.68
  50.2 4.9 %mul.69 = f32[1536,512]{1,0:T(8,128)} reshape(f32[384,4,512]{2,1,0:T(4,128)} %mul.68) | data formatting | bytes 6291456 | tf_op jit(solution)/shard_map/mul | solution.py:99
  55.1 44.7 %all-to-all-done.1 = bf16[8,384,512]{2,1,0:T(8,128)(2,1)} async-done(((bf16[8,384,512]{2,1,0:T(8,128)(2,1)}), bf16[8,384,512]{2,1,0:T(8,128)(2,1)}, u32[]{:S(2)}, u32[]{:S(2)}) %all-to-all-start.1) | async-done | bytes 3145760 | tf_op jit(solution)/shard_map/all_to_all | solution.py:50
  99.8 7.8 %gather_fusion.1 = bf16[1536,512]{1,0:T(8,128)(2,1)} fusion(bf16[3072,512]{1,0:T(8,128)(2,1)} %bitcast.7, s32[2048]{0:T(1024)S(1)} %pad_clamp_fusion), kind=kCustom, calls=%fused_computation.1 | custom fusion | bytes 3151872 | tf_op jit(solution)/shard_map/gather | solution.py:51
  107.6 3.5 %reshape.274 = bf16[384,4,512]{2,1,0:T(4,128)(2,1)} reshape(bf16[1536,512]{1,0:T(8,128)(2,1)} %gather_fusion.1) | data formatting | bytes 3145728 | tf_op jit(solution)/shard_map/reshape | solution.py:51
  111.1 2.8 fusion.18
  113.9 0.1 copy.17
  114.1 0.2 copy.18
  114.3 2.4 fusion.43
  116.8 34.0 %while.14 = (s32[]{:T(128)}, f32[384]{0:T(512)S(1)}, f32[384]{0:T(512)S(1)}, f32[384,512]{1,0:T(8,128)S(1)}, bf16[8,1024,512]{2,1,0:T(8,128)(2,1)}, /*index=5*/bf16[384,512]{1,0:T(8,128)(2,1)S(1)}, s32[]{:T(128)}) while((s32[]{:T(128)}, f32[384]{0:T(512)S(1)}, f32[384]{0:T(512)S(1)}, f32[384,512]{1,0:T(8,128)S(1)}, ...), condition=%wide.region_10.11_spmd, body=%wide.region_7.10_spmd.sunk | while | flops 808059648 | bytes 8806493 | solution.py:79
  116.8 2.0 fusion.59
  118.8 0.3 fusion.60
  119.1 1.9 convolution_add_fusion.2
  121.1 2.0 fusion.59
  123.0 0.3 fusion.60
  123.3 1.9 convolution_add_fusion.2
  125.3 2.0 fusion.59
  127.3 0.3 fusion.60
  127.6 1.9 convolution_add_fusion.2
  129.6 2.0 fusion.59
  131.5 0.3 fusion.60
  131.8 1.9 convolution_add_fusion.2
  133.8 2.0 fusion.59
  135.8 0.3 fusion.60
  136.1 1.9 convolution_add_fusion.2
  138.1 2.0 fusion.59
  140.0 0.3 fusion.60
  140.4 1.9 convolution_add_fusion.2
  142.3 2.0 fusion.59
  144.3 0.3 fusion.60
  144.6 1.9 convolution_add_fusion.2
  146.6 2.0 fusion.59
  148.5 0.3 fusion.60
  148.9 1.9 convolution_add_fusion.2
  150.9 0.1 copy.14
  151.0 0.1 mul.66
  151.2 10.7 %scatter_custom_fusion.1 = bf16[3072,512]{1,0:T(8,128)(2,1)} fusion(s32[1536]{0:T(1024)S(1)} %fusion.31, f32[1536,512]{1,0:T(8,128)} %mul.69, f32[]{:T(128)} %constant.84.clone.1, f32[1536]{0:T(1024)S(1)} %mul.66, bf16[]{:T(256)} %constant.87.clone.1), kind=kCustom, calls=%fused_computation.23 | custom fusion | flops 2359296 | bytes 6299654 | tf_op jit(solution)/shard_map/scatter | solution.py:104
  161.9 4.4 %all-to-all-start.2 = ((bf16[8,384,512]{2,1,0:T(8,128)(2,1)}), bf16[8,384,512]{2,1,0:T(8,128)(2,1)}, u32[]{:S(2)}, u32[]{:S(2)}) async-start(bf16[8,384,512]{2,1,0:T(8,128)(2,1)} %bitcast.82), calls=%async_computation.2 | async-start | bytes 6291456 | tf_op jit(solution)/shard_map/all_to_all | solution.py:106
  166.4 2.0 slice.22
  168.4 1.4 multiply_reduce_fusion
  169.9 1.7 convolution_bitcast_fusion
  171.6 0.3 all-reduce.5.cloned.1.call-start
  171.9 68.9 %all-reduce.3.cloned.1.call-done = f32[512,512]{0,1:T(8,128)} async-done(((f32[512,512]{0,1:T(8,128)}), f32[512,512]{0,1:T(8,128)}) %all-reduce.3.cloned.1.call-update) | async-done | bytes 1048592 | tf_op jit(solution)/shard_map/psum | solution.py:114
  240.8 0.6 subtract_reduce_fusion
  241.4 12.5 %psum.30 = f32[]{:T(128)} all-reduce(f32[]{:T(128)} %subtract_reduce_fusion), channel_id=1, replica_groups=mesh['dp'=4,'lib'=8] {'lib'}, use_global_device_ids=true, to_apply=%region_17.18 | all-reduce | flops 1 | bytes 8 | tf_op jit(solution)/shard_map/psum | solution.py:114
  253.9 13.2 %psum.31 = f32[]{:T(128)} all-reduce(f32[]{:T(128)} %psum.30), channel_id=1, replica_groups=mesh['dp'=4,'lib'=8] {'dp'}, use_global_device_ids=true, to_apply=%region_18.19 | all-reduce | flops 1 | bytes 8 | tf_op jit(solution)/shard_map/psum | solution.py:114
  267.7 26.9 %all-reduce.5.cloned.1.call-done = f32[512,512]{0,1:T(8,128)} async-done(((f32[512,512]{0,1:T(8,128)}), f32[512,512]{0,1:T(8,128)}) %all-reduce.5.cloned.1.call-update) | async-done | bytes 1048592 | tf_op jit(solution)/shard_map/psum | solution.py:114
  294.6 2.5 copy.15
  297.1 23.2 %scatter_custom_fusion.2 = f32[2048,512]{1,0:T(8,128)} fusion(s32[3072]{0:T(1024)S(1)} %bitcast.88, bf16[3072,512]{1,0:T(8,128)(2,1)} %bitcast.19, f32[]{:T(128)} %constant.73.clone.1), kind=kCustom, calls=%fused_computation.19 | custom fusion | flops 3145728 | bytes 7340036 | tf_op jit(solution)/shard_map/scatter-add | solution.py:112
  (61 shorter events, 0.9 us)
Async XLA Ops:
  7.2 21.2 %copy-start = (bf16[2048,512]{1,0:T(8,128)(2,1)S(1)}, bf16[2048,512]{1,0:T(8,128)(2,1)}, u32[]{:S(2)}) copy-start(bf16[2048,512]{1,0:T(8,128)(2,1)} %param.11) | copy-start | bytes 6291460
  7.2 109.6 %all-gather.2.cloned.1.call-start = ((), (), s32[]{:S(2)}) async-start(), calls=%async_computation.3 | async-start | bytes 9437184 | tf_op jit(solution)/shard_map/all_gather | solution.py:73
  41.7 4.8 %copy-start.3 = (bf16[512,512]{1,0:T(8,128)(2,1)S(1)}, bf16[512,512]{1,0:T(8,128)(2,1)}, u32[]{:S(2)}) copy-start(bf16[512,512]{1,0:T(8,128)(2,1)} %param.9) | copy-start | bytes 1572868
  41.7 4.8 %copy-start.4 = (bf16[384,512]{1,0:T(8,128)(2,1)S(1)}, bf16[384,512]{1,0:T(8,128)(2,1)}, u32[]{:S(2)}) copy-start(bf16[384,512]{1,0:T(8,128)(2,1)} %param.8) | copy-start | bytes 1179652
  41.7 58.1 %all-to-all-start.1 = ((bf16[8,384,512]{2,1,0:T(8,128)(2,1)}), bf16[8,384,512]{2,1,0:T(8,128)(2,1)}, u32[]{:S(2)}, u32[]{:S(2)}) async-start(bf16[8,384,512]{2,1,0:T(8,128)(2,1)} %bitcast.83), calls=%async_computation.1 | async-start | bytes 6291456 | tf_op jit(solution)/shard_map/all_to_all | solution.py:50
  47.1 0.9 copy-start.1
  111.1 2.9 copy-start.6
  161.9 135.2 %all-to-all-start.2 = ((bf16[8,384,512]{2,1,0:T(8,128)(2,1)}), bf16[8,384,512]{2,1,0:T(8,128)(2,1)}, u32[]{:S(2)}, u32[]{:S(2)}) async-start(bf16[8,384,512]{2,1,0:T(8,128)(2,1)} %bitcast.82), calls=%async_computation.2 | async-start | bytes 6291456 | tf_op jit(solution)/shard_map/all_to_all | solution.py:106
  166.3 3.5 %copy-start.5 = (bf16[384,512]{1,0:T(8,128)(2,1)S(1)}, bf16[384,512]{1,0:T(8,128)(2,1)}, u32[]{:S(2)}) copy-start(bf16[384,512]{1,0:T(8,128)(2,1)} %param.8) | copy-start | bytes 1179652
  166.3 74.4 %all-reduce.3.cloned.1.call-start = ((), (), s32[]{:S(2)}) async-start(), calls=%async_computation.4 | async-start | bytes 2097152 | tf_op jit(solution)/shard_map/psum | solution.py:114
  166.4 3.5 %copy-start.2 = (f32[384,512]{1,0:T(8,128)S(1)}, f32[384,512]{1,0:T(8,128)}, u32[]{:S(2)}) copy-start(f32[384,512]{1,0:T(8,128)} %copy-done.1) | copy-start | bytes 2359300
  171.6 123.0 %all-reduce.5.cloned.1.call-start = ((), (), s32[]{:S(2)}) async-start(), calls=%async_computation.5 | async-start | bytes 2097152 | tf_op jit(solution)/shard_map/psum | solution.py:114
Sparse Core Ops, SparseCore 0:
  9.9 81.2 all-gather.1
  171.7 68.9 all-reduce.2
  243.1 51.3 all-reduce.4
